TPU v7x, 512 devices: a whole 4x4x16 slice. The times are simulated.
512 devices in a mesh: row: 32 (over x_lo, z), col: 16 (over y, x_hi, core).
Axes of the slice: x: 4 (x_hi: 2, x_lo: 2; x = x_hi * 2 + x_lo), y: 4, z: 16, core: 2. Of those that a mesh axis runs over, the one named last changes fastest.
Arguments:
- snapshots: float32 [65536, 4096], P('row', 'col'), may hold values from -260 to 260
Outputs:
- rotated: float32 [65536, 4096], P('row', 'col')
All inputs are finite; a program needn't handle non-finite values.
Results may differ from a plain program's by a relative error of at most 0.0003.
Values sent between devices are 32-bit elements; how exact they have to be, the bound alone decides.
A program may use at most 64 MiB of HBM per device.

v0:
```python
import jax
import jax.numpy as jnp
import numpy as np
from jax import lax
from jax.sharding import PartitionSpec as P

INNER_ROUNDS = 10


def passed_along(block, axis, distance):
    devices = range(lax.axis_size(axis))
    route = [(i - distance, i) for i in devices if i - distance in devices]
    return lax.ppermute(block, axis, route)


def round_tables(width, count):
    partner = np.zeros((count, width), np.int32)
    first = np.zeros((count, width), np.bool_)
    for turn in range(count):
        start = turn % (width - 1)
        pairs = [(start, width - 1)]
        for step in range(1, width // 2):
            pairs.append(((start + step) % (width - 1), (start - step) % (width - 1)))
        for left, right in pairs:
            lower, upper = (min(left, right), max(left, right))
            partner[turn, lower] = upper
            partner[turn, upper] = lower
            first[turn, lower] = True
    return (partner, first)


def dot_high(left, right):
    return jnp.dot(left, right, precision=lax.Precision.HIGHEST, preferred_element_type=jnp.float32)


def jacobi(gram, count):
    width = gram.shape[0]
    partner_np, first_np = round_tables(width, count)
    partner = jnp.asarray(partner_np)
    first = jnp.asarray(first_np)
    places = lax.broadcasted_iota(jnp.int32, (width, width), 0)
    identity = jnp.eye(width, dtype=jnp.float32)

    def turn(index, state):
        matrix, basis = state
        other = partner[index]
        lead = first[index]
        pick = (places == other[None, :]).astype(jnp.float32)
        diag = jnp.sum(matrix * identity, axis=0)
        diag_other = jnp.sum(diag[:, None] * pick, axis=0)
        cross = jnp.sum(matrix * pick, axis=0)
        cross_other = jnp.sum(cross[:, None] * pick, axis=0)
        gamma = jnp.where(lead, cross, cross_other)
        gap = jnp.where(lead, diag - diag_other, diag_other - diag)
        sigma = jnp.where(gap >= 0, 1.0, -1.0).astype(jnp.float32)
        theta = 0.5 * jnp.arctan2(-2.0 * gamma * sigma, jnp.abs(gap))
        cosine = jnp.cos(theta)
        sine = jnp.sin(theta)
        factor = jnp.where(lead, -sine, sine)
        rotation = identity * cosine[None, :] + pick * factor[None, :]
        matrix = dot_high(matrix, rotation)
        matrix = dot_high(rotation.T, matrix)
        basis = dot_high(basis, rotation)
        return (matrix, basis)

    start = (gram, identity)
    return lax.fori_loop(0, count, turn, start)


def inner_product(left, right):
    return lax.dot_general(
        left,
        right,
        (((0,), (0,)), ((), ())),
        precision=lax.Precision.HIGHEST,
        preferred_element_type=jnp.float32,
    )


def pair_gram(top, bottom):
    joined = jnp.concatenate([top, bottom], 1)
    return lax.psum(inner_product(joined, joined), "row")


def rotate(top, bottom, gram):
    half = top.shape[1]
    matrix, basis = jacobi(gram, INNER_ROUNDS)
    new_top = dot_high(top, basis[:half, :half]) + dot_high(bottom, basis[half:, :half])
    new_bottom = dot_high(top, basis[:half, half:]) + dot_high(bottom, basis[half:, half:])
    return (new_top, new_bottom, matrix)


def local(snapshots):
    half = snapshots.shape[1] // 2
    position = lax.axis_index("col")
    cycle = lax.axis_size("col")
    is_head = position == 0
    is_tail = position == cycle - 1
    top = snapshots[:, :half]
    bottom = snapshots[:, half:]
    top, bottom, matrix = rotate(top, bottom, pair_gram(top, bottom))
    send_top = jnp.where(is_head, bottom, top)
    got_top = passed_along(send_top, "col", 1)
    got_bottom = passed_along(bottom, "col", -1)
    next_top = jnp.where(is_head, top, got_top)
    next_bottom = jnp.where(is_tail, top, got_bottom)
    gram = pair_gram(next_top, next_bottom)
    final_top, final_bottom, matrix = rotate(next_top, next_bottom, gram)
    return jnp.concatenate([final_top, final_bottom], 1)


def solution(mesh):
    return jax.shard_map(
        local,
        mesh=mesh,
        in_specs=(P("row", "col"),),
        out_specs=P("row", "col"),
        check_vma=False,
    )
```

profile of v0, /device:TPU:8, one launch (start us, length us, event | category | flops | bytes accessed | tf_op | source)
XLA Modules:
  0.0 682.4 jit_solution(3021937310409336629)
XLA Ops:
  6.5 6.4 fusion.100
  13.1 258.8 %all-reduce.3.cloned.1.call-done = f32[256,256]{1,0:T(8,128)} async-done(((f32[256,256]{1,0:T(8,128)}), f32[256,256]{1,0:T(8,128)}) %all-reduce.3.cloned.1.call-update) | async-done | bytes 262160 | tf_op jit(solution)/shard_map/psum | solution.py:82
  271.9 55.6 %while.36 = (s32[]{:T(128)}, f32[256,256]{1,0:T(8,128)}, f32[256,256]{0,1:T(8,128)S(1)}, s32[]{:T(128)}, pred[10,256]{1,0:T(8,128)(4,1)S(1)}, /*index=5*/s32[10,256]{1,0:T(8,128)}) while((s32[]{:T(128)}, f32[256,256]{1,0:T(8,128)}, f32[256,256]{0,1:T(8,128)S(1)}, s32[]{:T(128)}, ...), condition=%wide.region_6.7_spmd.clone.clone.clone, body=%wide.region_1.6_spmd.sunk.clone.clone.clone.sunk | while | flops 605685760 | bytes 2391641 | solution.py:67
  272.7 1.0 select_reduce_fusion.4
  274.1 1.5 fusion.135
  275.6 1.3 fusion.136
  278.3 1.0 select_reduce_fusion.4
  279.6 1.5 fusion.135
  281.2 1.3 fusion.136
  285.2 1.5 fusion.135
  286.7 1.3 fusion.136
  290.7 1.5 fusion.135
  292.3 1.3 fusion.136
  296.3 1.5 fusion.135
  297.8 1.3 fusion.136
  301.8 1.5 fusion.135
  303.4 1.3 fusion.136
  307.3 1.5 fusion.135
  308.9 1.3 fusion.136
  312.9 1.5 fusion.135
  314.4 1.3 fusion.136
  318.4 1.5 fusion.135
  320.0 1.3 fusion.136
  324.0 1.5 fusion.135
  325.5 1.3 fusion.136
  327.5 1.0 fusion.80
  328.5 1.0 fusion.82
  329.5 1.0 fusion.73
  330.6 2.5 broadcast_select_fusion.2
  333.1 1.9 collective-permute-start
  335.0 6.2 collective-permute-start.1
  341.2 17.8 %collective-permute-done = f32[2048,128]{0,1:T(8,128)S(1)} collective-permute-done((f32[2048,128]{0,1:T(8,128)}, f32[2048,128]{0,1:T(8,128)S(1)}, u32[]{:S(2)}, u32[]{:S(2)}) %collective-permute-start) | collective-permute-done | bytes 1048608 | tf_op jit(solution)/shard_map/ppermute | solution.py:13
  359.0 2.0 collective-permute-done.1
  360.9 1.7 broadcast_select_fusion.1
  362.6 2.6 fusion.74
  365.2 248.6 %all-reduce.5.cloned.1.call-done = f32[256,256]{1,0:T(8,128)} async-done(((f32[256,256]{1,0:T(8,128)}), f32[256,256]{1,0:T(8,128)}) %all-reduce.5.cloned.1.call-update) | async-done | bytes 262160 | tf_op jit(solution)/shard_map/psum | solution.py:82
  613.9 55.4 %while.37 = (s32[]{:T(128)}, f32[256,256]{1,0:T(8,128)}, f32[256,256]{0,1:T(8,128)S(1)}, s32[]{:T(128)}, pred[10,256]{1,0:T(8,128)(4,1)S(1)}, /*index=5*/s32[10,256]{1,0:T(8,128)}) while((s32[]{:T(128)}, f32[256,256]{1,0:T(8,128)}, f32[256,256]{0,1:T(8,128)S(1)}, s32[]{:T(128)}, ...), condition=%wide.region_13.14_spmd.clone.clone.clone, body=%wide.region_8.13_spmd.sunk.clone.clone.clone.sunk | while | flops 605685760 | bytes 2391641 | solution.py:67
  615.9 1.5 fusion.143
  617.5 1.3 fusion.144
  621.5 1.5 fusion.143
  623.0 1.3 fusion.144
  627.0 1.5 fusion.143
  628.6 1.3 fusion.144
  632.6 1.5 fusion.143
  634.1 1.3 fusion.144
  636.8 1.0 select_reduce_fusion.5
  638.1 1.5 fusion.143
  639.7 1.3 fusion.144
  643.7 1.5 fusion.143
  645.2 1.3 fusion.144
  647.9 1.0 select_reduce_fusion.5
  649.2 1.5 fusion.143
  650.8 1.3 fusion.144
  654.7 1.5 fusion.143
  656.3 1.3 fusion.144
  660.3 1.5 fusion.143
  661.8 1.3 fusion.144
  665.8 1.5 fusion.143
  667.4 1.3 fusion.144
  669.3 1.1 fusion.85
  670.4 1.1 fusion.88
  671.4 1.1 convolution_add_fusion.1
  672.5 1.1 convolution_add_fusion
  673.8 1.8 copy.6
  (169 shorter events, 49.4 us)
Async XLA Ops:
  6.5 265.3 %copy-start.2 = (pred[10,256]{1,0:T(8,128)(4,1)S(1)}, pred[10,256]{1,0:T(8,128)(4,1)}, u32[]{:S(2)}) copy-start(pred[10,256]{1,0:T(8,128)(4,1)} %constant.143.clone..sunk.8) | copy-start | bytes 7684
  6.5 265.3 %all-reduce.3.cloned.1.call-start = ((), (), s32[]{:S(2)}) async-start(), calls=%async_computation | async-start | bytes 524288 | tf_op jit(solution)/shard_map/psum | solution.py:82
  13.0 600.9 %all-reduce.5.cloned.1.call-start = ((), (), s32[]{:S(2)}) async-start(), calls=%async_computation.1 | async-start | bytes 524288 | tf_op jit(solution)/shard_map/psum | solution.py:82
  271.9 55.6 %copy-start = (f32[2048,256]{1,0:T(8,128)S(1)}, f32[2048,256]{1,0:T(8,128)}, u32[]{:S(2)}) copy-start(f32[2048,256]{1,0:T(8,128)} %param.9) | copy-start | bytes 6291460
  330.6 2.5 copy-start.1
  333.1 25.9 %collective-permute-start = (f32[2048,128]{0,1:T(8,128)}, f32[2048,128]{0,1:T(8,128)S(1)}, u32[]{:S(2)}, u32[]{:S(2)}) collective-permute-start(f32[2048,128]{0,1:T(8,128)} %get-tuple-element.387), channel_id=1, source_target_pairs={{0,1},{1,2},{2,3},{3,4},{4,5},{5,6},{6,7},{7,8},{8,9},{9,10},{10,1... | collective-permute-start | bytes 3145736 | tf_op jit(solution)/shard_map/ppermute | solution.py:13
  335.0 25.9 %collective-permute-start.1 = (f32[2048,128]{0,1:T(8,128)}, f32[2048,128]{0,1:T(8,128)}, u32[]{:S(2)}, u32[]{:S(2)}) collective-permute-start(f32[2048,128]{0,1:T(8,128)} %get-tuple-element.388), channel_id=1, source_target_pairs={{1,0},{2,1},{3,2},{4,3},{5,4},{6,5},{7,6},{8,7},{9,8},{10,9},{11,1... | collective-permute-start | bytes 3145736 | tf_op jit(solution)/shard_map/ppermute | solution.py:13
Sparse Core Ops, SparseCore 0:
  13.1 258.7 all-reduce.2
  365.4 248.4 all-reduce.4
where the time goes:
time: 685 us; the launch traced here: 682 us
  waiting for transfers between devices  527 us (77%)
  matrix products  87.6 us (13%)
  other arithmetic  28.4 us (4%)
  local copies, waits for them, and re-layouts  16.5 us (2%)
  between operations  13.5 us (2%)
  starting transfers between devices  8.18 us (1%)
    psum x2, waiting for transfers between devices, pair_gram(): return lax.psum(inner_product(joined, joined), 'row')  507 us
    dot_general x68, matrix products, dot_high(): jnp.dot(left, right, precision=lax.Precision.HIGHEST, preferred_element_t...  78.6 us
    reduce_sum x20, other arithmetic, turn(): diag = jnp.sum(matrix * identity, axis=0)  20.4 us
    ppermute x2, waiting for transfers between devices, passed_along(): return lax.ppermute(block, axis, route)  19.7 us
    dynamic_slice x20, local copies, waits for them, and re-layouts, turn(): other = partner[index]  14.3 us
  transfers between devices with their start and end apart: 4, of which 4 were waited for; matrix products, arithmetic and copies ran while one was open for 0% of the time, Pallas kernels for 0%

commit v1 on v0

v1 whole, which is shorter than its diff:
```python
import functools

import jax
import jax.numpy as jnp
from jax import lax
from jax.experimental import pallas as pl
from jax.experimental.pallas import tpu as pltpu
from jax.sharding import PartitionSpec as P

INNER_ROUNDS = 10
HALF = 128
CHUNK = 256
MESH = pl.DeviceIdType.MESH
F32 = jnp.float32
BF16 = jnp.bfloat16


def split(value):
    high = value.astype(BF16)
    return high, (value - high.astype(F32)).astype(BF16)


def dot(left, right):
    return jnp.dot(left, right, preferred_element_type=F32)


def dot_rows(left, right):
    return lax.dot_general(left, right, (((0,), (0,)), ((), ())), preferred_element_type=F32)


def exact(left, right):
    return jnp.dot(left, right, precision=lax.Precision.HIGHEST, preferred_element_type=F32)


def iota(shape, axis):
    return lax.broadcasted_iota(jnp.int32, shape, axis)


def reversal():
    return (iota((HALF, HALF), 0) + iota((HALF, HALF), 1) == HALF - 1).astype(F32)


def shifted(first, second, axis):
    place = iota(first.shape, axis)
    mixed = jnp.where(place == 0, first, second)
    new_first = jnp.where(place == HALF - 1, second, pltpu.roll(first, HALF - 1, axis))
    new_second = jnp.where(place == 0, second, pltpu.roll(mixed, 1, axis))
    return new_first, new_second


def angles(diag_first, diag_second, cross, turn):
    slot = iota((1, HALF), 1)
    upper = jnp.where(slot == 0, 2 * HALF - 1, jnp.where(turn >= slot, turn - slot, turn - slot + 2 * HALF - 1))
    lead = turn + slot < upper
    gap = diag_first - diag_second
    gap_lead = jnp.where(lead, gap, -gap)
    height = jnp.where(gap_lead >= 0, -2.0, 2.0) * cross
    width = jnp.abs(gap)
    tall = jnp.abs(height)
    big = jnp.maximum(width, tall)
    safe = jnp.where(big > 0, big, 1.0)
    ratio = jnp.minimum(width, tall) / safe
    total = width + big * jnp.sqrt(1.0 + ratio * ratio)
    tangent = height / jnp.where(total > 0, total, 1.0)
    cosine = 1.0 / jnp.sqrt(1.0 + tangent * tangent)
    sine = tangent * cosine
    return cosine, jnp.where(lead, -sine, sine)


def solve(tt, tb, bb, work, basis):
    flip = reversal()
    tb = exact(tb, flip)
    work[0] = tt
    work[1] = tb
    work[2] = tb.T
    work[3] = exact(flip, exact(bb, flip))
    basis[0] = (iota((2 * HALF, HALF), 0) == iota((2 * HALF, HALF), 1)).astype(F32)
    basis[1] = (iota((2 * HALF, HALF), 0) + iota((2 * HALF, HALF), 1) == 2 * HALF - 1).astype(F32)

    def turn(index, carry):
        eye = iota((HALF, HALF), 0) == iota((HALF, HALF), 1)
        tt, tb, bt, bb = work[0], work[1], work[2], work[3]

        def diagonal(block):
            return jnp.sum(jnp.where(eye, block, 0.0), axis=0, keepdims=True)

        cosine, factor = angles(diagonal(tt), diagonal(bb), diagonal(tb), index)
        cosine_rows = jnp.broadcast_to(cosine, (HALF, HALF)).T
        factor_rows = jnp.broadcast_to(factor, (HALF, HALF)).T
        tt, tb = tt * cosine + tb * factor, tb * cosine - tt * factor
        bt, bb = bt * cosine + bb * factor, bb * cosine - bt * factor
        tt, bt = tt * cosine_rows + bt * factor_rows, bt * cosine_rows - tt * factor_rows
        tb, bb = tb * cosine_rows + bb * factor_rows, bb * cosine_rows - tb * factor_rows
        tt, tb = shifted(tt, tb, 1)
        bt, bb = shifted(bt, bb, 1)
        tt, bt = shifted(tt, bt, 0)
        tb, bb = shifted(tb, bb, 0)
        work[0], work[1], work[2], work[3] = tt, tb, bt, bb
        first, second = basis[0], basis[1]
        first, second = first * cosine + second * factor, second * cosine - first * factor
        basis[0], basis[1] = shifted(first, second, 1)
        return carry

    lax.fori_loop(0, INNER_ROUNDS, turn, 0)

    count = 2 * HALF - 1
    slot = iota((HALF, 2 * HALF), 0)
    natural = iota((HALF, 2 * HALF), 1)
    back = INNER_ROUNDS - slot
    place = jnp.where(slot == 0, count, jnp.where(back >= 0, back, back + count))
    first_place = natural == slot + INNER_ROUNDS
    second_place = natural == place

    high = []
    for part in zip(split(basis[0]), split(basis[1])):
        high.append((dot(part[0], first_place.astype(BF16)) + dot(part[1], second_place.astype(BF16))).astype(BF16))

    def turned():
        a, b = first_place.astype(F32), second_place.astype(F32)
        upper = exact(work[0], a) + exact(work[1], b)
        lower = exact(work[2], a) + exact(work[3], b)

        def block(columns):
            left = slice(columns * HALF, (columns + 1) * HALF)
            return exact(a[:, left].T, upper[:, left]) + exact(b[:, left].T, lower[:, left])

        return block(0), block(1)

    return high[0], high[1], turned


def times_basis(high, low, basis_high, basis_low):
    return dot(high, basis_high) + dot(low, basis_high) + dot(high, basis_low)


class Sum:
    def __init__(self, mine, parts, total, sems, n):
        self.mine, self.parts, self.total, self.sems, self.n = mine, parts, total, sems, n
        self.me = lax.axis_index("row")

    def each(self, action):
        def step(i, carry):
            peer = lax.rem(self.me + i, self.n)
            action(peer)
            return carry

        lax.fori_loop(1, self.n, step, 0)

    def drain(self, source, index):
        view = source.at[pl.ds(0, self.n - 1)]
        pltpu.make_async_copy(view, view, self.sems.at[index]).wait()

    def scatter(self):
        self.each(
            lambda peer: pltpu.make_async_remote_copy(
                src_ref=self.mine.at[peer],
                dst_ref=self.parts.at[self.me],
                send_sem=self.sems.at[0],
                recv_sem=self.sems.at[1],
                device_id={"row": peer},
                device_id_type=MESH,
            ).start()
        )
        self.parts[self.me] = self.mine[self.me]

    def add(self):
        self.drain(self.parts, 1)
        total = self.parts[0]
        for i in range(1, self.n):
            total = total + self.parts[i]
        return total

    def gather(self, piece):
        self.total[self.me] = piece
        self.each(
            lambda peer: pltpu.make_async_remote_copy(
                src_ref=self.total.at[self.me],
                dst_ref=self.total.at[self.me],
                send_sem=self.sems.at[2],
                recv_sem=self.sems.at[3],
                device_id={"row": peer},
                device_id_type=MESH,
            ).start()
        )
        self.drain(self.total, 3)

    def finish(self):
        self.drain(self.mine, 0)
        self.drain(self.total, 2)


def kernel(
    n, cycle, x_hbm, t2, b2, w_ref,
    x, xh, xl, left, right, gram,
    mine1, parts1, total1, mine2, parts2, total2,
    work, basis, blocks, got_blocks,
    load_sems, sums1, sums2, block_sems, chunk_sems,
):
    row, col = lax.axis_index("row"), lax.axis_index("col")
    rows = x.shape[0]
    chunks = rows // CHUNK
    is_head, is_tail = col == 0, col == cycle - 1

    def load(c):
        where = pl.ds(c * CHUNK, CHUNK)
        return pltpu.make_async_copy(x_hbm.at[where], x.at[where], load_sems.at[c])

    for c in range(chunks):
        load(c).start()

    barrier = pltpu.get_barrier_semaphore()

    def greet(i, carry):
        pl.semaphore_signal(barrier, inc=1, device_id={"row": lax.rem(row + i, n)}, device_id_type=MESH)
        return carry

    lax.fori_loop(1, n, greet, 0)

    @pl.when(jnp.logical_not(is_tail))
    def _():
        pl.semaphore_signal(barrier, inc=1, device_id={"col": col + 1}, device_id_type=MESH)

    @pl.when(jnp.logical_not(is_head))
    def _():
        pl.semaphore_signal(barrier, inc=1, device_id={"col": col - 1}, device_id_type=MESH)

    gram[...] = jnp.zeros_like(gram)
    for c in range(chunks):
        load(c).wait()
        where = pl.ds(c * CHUNK, CHUNK)
        high, low = split(x[where])
        xh[where] = high
        xl[where] = low
        gram[0] += dot_rows(high, high) + dot_rows(low, low)
        gram[1] += dot_rows(high, low)
    full = gram[0] + (gram[1] + gram[1].T)
    tt, tb, bb = full[:HALF, :HALF], full[:HALF, HALF:], full[HALF:, HALF:]
    below = iota((HALF, HALF), 0) >= iota((HALF, HALF), 1)
    eye = iota((HALF, HALF), 0) == iota((HALF, HALF), 1)
    folded = jnp.where(below, tt, bb)
    size1 = 2 * HALF // n
    mine1[:, :size1] = jnp.concatenate([tb, folded], 0).reshape(n, size1, HALF)
    corner = jnp.sum(jnp.where(eye, bb, 0.0), axis=0, keepdims=True)
    mine1[:, size1:] = jnp.broadcast_to(corner[None], (n, 1, HALF))

    inner = jnp.logical_not(jnp.logical_or(is_head, is_tail))

    @pl.when(inner)
    def _():
        pl.semaphore_wait(barrier, n + 1)

    @pl.when(jnp.logical_not(inner))
    def _():
        pl.semaphore_wait(barrier, n)

    sum1 = Sum(mine1, parts1, total1, sums1, n)
    sum1.scatter()
    piece = sum1.add()
    corner = piece[size1:]
    sum1.gather(piece[:size1])
    whole = total1[...].reshape(2 * HALF, HALF)
    tb, folded = whole[:HALF], whole[HALF:]
    turned_fold = folded.T
    tt = jnp.where(below, folded, turned_fold)
    bb = jnp.where(below, turned_fold, folded)
    bb = jnp.where(eye, jnp.broadcast_to(corner, (HALF, HALF)), bb)

    basis_high, basis_low, turned = solve(tt, tb, bb, work, basis)

    def send(kind, c):
        if c is None:
            source, target, sems = blocks.at[kind], got_blocks.at[kind], block_sems
            index = kind
        else:
            where = pl.ds(c * CHUNK, CHUNK)
            source = (right if kind == 0 else left).at[where]
            target = (t2 if kind == 0 else b2).at[where]
            sems = chunk_sems
            index = kind * chunks + c
        return pltpu.make_async_remote_copy(
            src_ref=source,
            dst_ref=target,
            send_sem=sems.at[0, index],
            recv_sem=sems.at[1, index],
            device_id={"col": col + 1 if kind == 0 else col - 1},
            device_id_type=MESH,
        )

    def start(c):
        @pl.when(jnp.logical_not(is_tail))
        def _():
            send(0, c).start()

        @pl.when(jnp.logical_not(is_head))
        def _():
            send(1, c).start()

    def arrive(c):
        @pl.when(jnp.logical_not(is_head))
        def _():
            send(0, c).wait_recv()

        @pl.when(jnp.logical_not(is_tail))
        def _():
            send(1, c).wait_recv()

    def left_device(c):
        @pl.when(jnp.logical_not(is_tail))
        def _():
            send(0, c).wait_send()

        @pl.when(jnp.logical_not(is_head))
        def _():
            send(1, c).wait_send()

    for c in range(chunks):
        where = pl.ds(c * CHUNK, CHUNK)
        moved = times_basis(xh[where], xl[where], basis_high, basis_low)
        top, bottom = moved[:, :HALF], moved[:, HALF:]
        right[where] = jnp.where(is_head, bottom, top)
        left[where] = bottom

        @pl.when(is_head)
        def _():
            t2[where] = top

        @pl.when(is_tail)
        def _():
            b2[where] = top

        start(c)

    tt, bb = turned()
    blocks[0] = jnp.where(is_head, bb, tt)
    blocks[1] = bb

    @pl.when(is_head)
    def _():
        got_blocks[0] = tt

    @pl.when(is_tail)
    def _():
        got_blocks[1] = tt

    start(None)
    gram[...] = jnp.zeros_like(gram)
    for c in range(chunks):
        arrive(c)
        where = pl.ds(c * CHUNK, CHUNK)
        th, tl = split(t2[where])
        bh, bl = split(b2[where])
        gram[0, :HALF, :HALF] += dot_rows(th, bh) + dot_rows(tl, bh) + dot_rows(th, bl)
    mine2[...] = gram[0, :HALF, :HALF].reshape(mine2.shape)
    sum2 = Sum(mine2, parts2, total2, sums2, n)
    sum2.scatter()
    sum2.gather(sum2.add())
    arrive(None)
    tb = total2[...].reshape(HALF, HALF)
    basis_high, basis_low, _ = solve(got_blocks[0], tb, got_blocks[1], work, basis)
    w_ref[0] = basis_high
    w_ref[1] = basis_low

    sum1.finish()
    sum2.finish()
    for c in range(chunks):
        left_device(c)
    left_device(None)


def last(t2, b2, w_ref, out):
    high, low = split(jnp.concatenate([t2[...], b2[...]], 1))
    out[...] = times_basis(high, low, w_ref[0], w_ref[1])


def local(n, cycle, snapshots):
    rows = snapshots.shape[0]
    chunks = rows // CHUNK
    dma = pltpu.SemaphoreType.DMA
    vmem = pl.BlockSpec(memory_space=pltpu.VMEM)
    size1, size2 = 2 * HALF // n, HALF // n
    t2, b2, w = pl.pallas_call(
        functools.partial(kernel, n, cycle),
        out_shape=[
            jax.ShapeDtypeStruct((rows, HALF), F32),
            jax.ShapeDtypeStruct((rows, HALF), F32),
            jax.ShapeDtypeStruct((2, 2 * HALF, 2 * HALF), BF16),
        ],
        in_specs=[pl.BlockSpec(memory_space=pl.ANY)],
        out_specs=[vmem] * 3,
        scratch_shapes=[
            pltpu.VMEM((rows, 2 * HALF), F32),
            pltpu.VMEM((rows, 2 * HALF), BF16),
            pltpu.VMEM((rows, 2 * HALF), BF16),
            pltpu.VMEM((rows, HALF), F32),
            pltpu.VMEM((rows, HALF), F32),
            pltpu.VMEM((2, 2 * HALF, 2 * HALF), F32),
            pltpu.VMEM((n, size1 + 1, HALF), F32),
            pltpu.VMEM((n, size1 + 1, HALF), F32),
            pltpu.VMEM((n, size1, HALF), F32),
            pltpu.VMEM((n, size2, HALF), F32),
            pltpu.VMEM((n, size2, HALF), F32),
            pltpu.VMEM((n, size2, HALF), F32),
            pltpu.VMEM((4, HALF, HALF), F32),
            pltpu.VMEM((2, 2 * HALF, HALF), F32),
            pltpu.VMEM((2, HALF, HALF), F32),
            pltpu.VMEM((2, HALF, HALF), F32),
            dma((chunks,)),
            dma((4,)),
            dma((4,)),
            dma((2, 2)),
            dma((2, 2 * chunks)),
        ],
        compiler_params=pltpu.CompilerParams(
            collective_id=0, has_side_effects=True, vmem_limit_bytes=40 << 20
        ),
    )(snapshots)
    return pl.pallas_call(
        last,
        grid=(rows // CHUNK,),
        out_shape=jax.ShapeDtypeStruct((rows, 2 * HALF), F32),
        in_specs=[
            pl.BlockSpec((CHUNK, HALF), lambda i: (i, 0)),
            pl.BlockSpec((CHUNK, HALF), lambda i: (i, 0)),
            pl.BlockSpec((2, 2 * HALF, 2 * HALF), lambda i: (0, 0, 0)),
        ],
        out_specs=pl.BlockSpec((CHUNK, 2 * HALF), lambda i: (i, 0)),
    )(t2, b2, w)


def solution(mesh):
    return jax.shard_map(
        functools.partial(local, mesh.shape["row"], mesh.shape["col"]),
        mesh=mesh,
        in_specs=(P("row", "col"),),
        out_specs=P("row", "col"),
        check_vma=False,
    )
```

time: 685 us -> 99.8 us (0.15)
  waiting for transfers between devices: 527 us -> 0 us
  Pallas kernels: 0 us -> 94.7 us
  matrix products: 87.6 us -> 0 us
  other arithmetic: 28.4 us -> 0 us
  between operations: 13.5 us -> 0.02 us
  local copies, waits for them, and re-layouts: 16.5 us -> 4.26 us
  starting transfers between devices: 8.18 us -> 0 us
    psum x2 -> x0, waiting for transfers between devices: 507 us -> none  [pair_gram(): return lax.psum(inner_product(joined, joined), 'row')]
    pallas_call x0 -> x2, Pallas kernels: none -> 94.7 us  [the longest x1 87.9 us: local(): pl.pallas_call(functools.partial(kernel, n, cycle), out_shape=[jax.ShapeD...]
    dot_general x70 -> x0, matrix products: 87.6 us -> none  [the longest x68 78.6 us: dot_high(): jnp.dot(left, right, precision=lax.Precision.HIGHEST, preferred_element_t...]
    reduce_sum x40 -> x0, other arithmetic: 23.3 us -> none  [the longest x20 20.4 us: turn(): diag = jnp.sum(matrix * identity, axis=0)]
    ppermute x2 -> x0, waiting for transfers between devices: 19.7 us -> none  [passed_along(): return lax.ppermute(block, axis, route)]
    dynamic_slice x20 -> x0, local copies, waits for them, and re-layouts: 14.3 us -> none  [turn(): other = partner[index]]
    ppermute x2 -> x0, starting transfers between devices: 8.14 us -> none  [passed_along(): return lax.ppermute(block, axis, route)]
  transfers between devices with their start and end apart: 4 -> 0, of which waited for: 4 -> 0; matrix products, arithmetic and copies ran while one was open for 0% -> 0% of each run, Pallas kernels for 0% -> 0%
where the time goes in v1:
time: 99.8 us; the launch traced here: 99 us
  Pallas kernels  94.7 us (95%)
  local copies, waits for them, and re-layouts  4.26 us (4%)
    pallas_call x1, Pallas kernels, local(): pl.pallas_call(functools.partial(kernel, n, cycle), out_shape=[jax.ShapeD...  87.9 us
    pallas_call x1, Pallas kernels, local(): pl.pallas_call(last, grid=(rows // CHUNK,), out_shape=jax.ShapeDtypeStruc...  6.78 us
    unnamed x8, local copies, waits for them, and re-layouts  4.26 us

profile of v1, /device:TPU:8, one launch (start us, length us, event | category | flops | bytes accessed | tf_op | source)
XLA Modules:
  0.0 99.0 jit_solution(12838057912987385831)
XLA Ops:
  0.0 0.0 copy-start
  0.0 1.6 %copy-done = f32[2048,256]{1,0:T(8,128)S(1)} copy-done((f32[2048,256]{1,0:T(8,128)S(1)}, f32[2048,256]{1,0:T(8,128)}, u32[]{:S(2)}) %copy-start) | copy-done | bytes 2097176
  1.6 87.9 %shard_map.17 = (f32[2048,128]{1,0:T(8,128)S(1)}, f32[2048,128]{1,0:T(8,128)S(1)}, bf16[2,256,256]{2,1,0:T(8,128)(2,1)S(1)}) custom-call(f32[2048,256]{1,0:T(8,128)S(1)} %copy-done), custom_call_target="tpu_custom_call" | custom-call | tf_op jit(solution)/shard_map/pallas_call | solution.py:381
  89.5 0.0 copy-start.1
  89.6 1.0 copy-done.1
  90.5 0.0 copy-start.2
  90.5 1.0 %copy-done.2 = f32[2048,128]{1,0:T(8,128)} copy-done((f32[2048,128]{1,0:T(8,128)}, f32[2048,128]{1,0:T(8,128)S(1)}, u32[]{:S(2)}) %copy-start.2) | copy-done | bytes 1048600
  91.5 0.0 copy-start.3
  91.5 0.7 copy-done.3
  92.2 6.8 %shard_map.18 = f32[2048,256]{1,0:T(8,128)} custom-call(f32[2048,128]{1,0:T(8,128)} %copy-done.1, f32[2048,128]{1,0:T(8,128)} %copy-done.2, bf16[2,256,256]{2,1,0:T(8,128)(2,1)} %copy-done.3), custom_call_target="tpu_custom_call" | custom-call | tf_op jit(solution)/shard_map/pallas_call | solution.py:417
Async XLA Ops:
  0.0 1.6 %copy-start = (f32[2048,256]{1,0:T(8,128)S(1)}, f32[2048,256]{1,0:T(8,128)}, u32[]{:S(2)}) copy-start(f32[2048,256]{1,0:T(8,128)} %x_hbm.1) | copy-start | bytes 6291460
  89.5 1.0 copy-start.1
  90.5 1.0 %copy-start.2 = (f32[2048,128]{1,0:T(8,128)}, f32[2048,128]{1,0:T(8,128)S(1)}, u32[]{:S(2)}) copy-start(f32[2048,128]{1,0:T(8,128)S(1)} %get-tuple-element.9.b2) | copy-start | bytes 3145732
  91.5 0.7 copy-start.3

commit v2 on v1

--- a/solution.py
+++ b/solution.py
@@ -139,12 +139,20 @@
         self.me = lax.axis_index("row")
 
     def each(self, action):
-        def step(i, carry):
-            peer = lax.rem(self.me + i, self.n)
-            action(peer)
+        half = self.n // 2
+        group, place = self.me // half, lax.rem(self.me, half)
+
+        def peer(k, other):
+            offset = half // 2 + (1 - 2 * lax.rem(k, 2)) * ((k + 1) // 2)
+            return lax.rem(group + other, 2) * half + lax.rem(place + offset, half)
+
+        def step(k, carry):
+            action(peer(k, 1))
+            action(peer(k, 0))
             return carry
 
-        lax.fori_loop(1, self.n, step, 0)
+        lax.fori_loop(0, half - 1, step, 0)
+        action(lax.rem(group + 1, 2) * half + place)
 
     def drain(self, source, index):
         view = source.at[pl.ds(0, self.n - 1)]
@@ -367,9 +375,20 @@
     left_device(None)
 
 
-def last(t2, b2, w_ref, out):
-    high, low = split(jnp.concatenate([t2[...], b2[...]], 1))
-    out[...] = times_basis(high, low, w_ref[0], w_ref[1])
+def last(t2, b2, w_ref, out, held, sems):
+    chunks = held.shape[0] // CHUNK
+
+    def store(c):
+        where = pl.ds(c * CHUNK, CHUNK)
+        return pltpu.make_async_copy(held.at[where], out.at[where], sems.at[c])
+
+    for c in range(chunks):
+        where = pl.ds(c * CHUNK, CHUNK)
+        high, low = split(jnp.concatenate([t2[where], b2[where]], 1))
+        held[where] = times_basis(high, low, w_ref[0], w_ref[1])
+        store(c).start()
+    for c in range(chunks):
+        store(c).wait()
 
 
 def local(n, cycle, snapshots):
@@ -385,7 +404,7 @@
             jax.ShapeDtypeStruct((rows, HALF), F32),
             jax.ShapeDtypeStruct((2, 2 * HALF, 2 * HALF), BF16),
         ],
-        in_specs=[pl.BlockSpec(memory_space=pl.ANY)],
+        in_specs=[pl.BlockSpec(memory_space=pltpu.HBM)],
         out_specs=[vmem] * 3,
         scratch_shapes=[
             pltpu.VMEM((rows, 2 * HALF), F32),
@@ -413,17 +432,14 @@
         compiler_params=pltpu.CompilerParams(
             collective_id=0, has_side_effects=True, vmem_limit_bytes=40 << 20
         ),
-    )(snapshots)
+    )(pltpu.with_memory_space_constraint(snapshots, pltpu.HBM))
     return pl.pallas_call(
         last,
-        grid=(rows // CHUNK,),
         out_shape=jax.ShapeDtypeStruct((rows, 2 * HALF), F32),
-        in_specs=[
-            pl.BlockSpec((CHUNK, HALF), lambda i: (i, 0)),
-            pl.BlockSpec((CHUNK, HALF), lambda i: (i, 0)),
-            pl.BlockSpec((2, 2 * HALF, 2 * HALF), lambda i: (0, 0, 0)),
-        ],
-        out_specs=pl.BlockSpec((CHUNK, 2 * HALF), lambda i: (i, 0)),
+        in_specs=[vmem] * 3,
+        out_specs=pl.BlockSpec(memory_space=pltpu.HBM),
+        scratch_shapes=[pltpu.VMEM((rows, 2 * HALF), F32), dma((chunks,))],
+        compiler_params=pltpu.CompilerParams(vmem_limit_bytes=24 << 20),
     )(t2, b2, w)
 
 

time: 99.8 us -> 83 us (0.83)
  the two profiles are of different devices: /device:TPU:8 before, /device:TPU:1 now
where the time goes in v2:
time: 83 us; the launch traced here: 82.8 us
  Pallas kernels  82.8 us (100%)
    pallas_call x1, Pallas kernels, local(): pl.pallas_call(functools.partial(kernel, n, cycle), out_shape=[jax.ShapeD...  80.9 us
    pallas_call x1, Pallas kernels, local(): pl.pallas_call(last, out_shape=jax.ShapeDtypeStruct((rows, 2 * HALF), F32...  1.91 us

profile of v2, /device:TPU:1, one launch (start us, length us, event | category | flops | bytes accessed | tf_op | source)
XLA Modules:
  0.0 82.8 jit_solution(12457628558836956194)
XLA Ops:
  0.0 80.9 %shard_map.17 = (f32[2048,128]{1,0:T(8,128)S(1)}, f32[2048,128]{1,0:T(8,128)S(1)}, bf16[2,256,256]{2,1,0:T(8,128)(2,1)S(1)}) custom-call(f32[2048,256]{1,0:T(8,128)} %x_hbm.1), custom_call_target="tpu_custom_call" | custom-call | tf_op jit(solution)/shard_map/pallas_call | solution.py:400
  80.9 1.9 %shard_map.18 = f32[2048,256]{1,0:T(8,128)} custom-call(f32[2048,128]{1,0:T(8,128)S(1)} %get-tuple-element.8.t2, f32[2048,128]{1,0:T(8,128)S(1)} %get-tuple-element.9.b2, bf16[2,256,256]{2,1,0:T(8,128)(2,1)S(1)} %get-tuple-element.10.w_ref), custom_call_target="tpu_custom_call" | custom-call | tf_op jit(solution)/shard_map/pallas_call | solution.py:436

commit v3 on v2

v3 whole, which is shorter than its diff:
```python
import functools

import jax
import jax.numpy as jnp
from jax import lax
from jax.experimental import pallas as pl
from jax.experimental.pallas import tpu as pltpu
from jax.sharding import PartitionSpec as P

INNER_ROUNDS = 10
HALF = 128
CHUNK = 256
EARLY = (1, 2)
SOLVE_ROWS = 64
MESH = pl.DeviceIdType.MESH
F32 = jnp.float32
BF16 = jnp.bfloat16


def split(value):
    high = value.astype(BF16)
    return high, (value - high.astype(F32)).astype(BF16)


def dot(left, right):
    return jnp.dot(left, right, preferred_element_type=F32)


def dot_rows(left, right):
    return lax.dot_general(left, right, (((0,), (0,)), ((), ())), preferred_element_type=F32)


def exact(left, right):
    return jnp.dot(left, right, precision=lax.Precision.HIGHEST, preferred_element_type=F32)


def exact_rows(left, right):
    return lax.dot_general(
        left, right, (((0,), (0,)), ((), ())), precision=lax.Precision.HIGHEST, preferred_element_type=F32
    )


def iota(shape, axis):
    return lax.broadcasted_iota(jnp.int32, shape, axis)


def reversal():
    return (iota((HALF, HALF), 0) + iota((HALF, HALF), 1) == HALF - 1).astype(F32)


def shifted(first, second, axis):
    place = iota(first.shape, axis)
    mixed = jnp.where(place == 0, first, second)
    new_first = jnp.where(place == HALF - 1, second, pltpu.roll(first, HALF - 1, axis))
    new_second = jnp.where(place == 0, second, pltpu.roll(mixed, 1, axis))
    return new_first, new_second


def angles(diag_first, diag_second, cross, turn):
    slot = iota((1, HALF), 1)
    upper = jnp.where(slot == 0, 2 * HALF - 1, jnp.where(turn >= slot, turn - slot, turn - slot + 2 * HALF - 1))
    lead = turn + slot < upper
    gap = diag_first - diag_second
    gap_lead = jnp.where(lead, gap, -gap)
    height = jnp.where(gap_lead >= 0, -2.0, 2.0) * cross
    width = jnp.abs(gap)
    big = jnp.maximum(width, jnp.abs(height))
    scale = 1.0 / jnp.where(big > 0, big, 1.0)
    width, height = width * scale, height * scale
    total = width + jnp.sqrt(width * width + height * height)
    tangent = height / jnp.where(big > 0, total, 1.0)
    cosine = lax.rsqrt(1.0 + tangent * tangent)
    sine = tangent * cosine
    return cosine, jnp.where(lead, -sine, sine)


def solve(tt, tb, bb, basis, image):
    basis[0] = (iota((2 * HALF, HALF), 0) == iota((2 * HALF, HALF), 1)).astype(F32)
    basis[1] = (iota((2 * HALF, HALF), 0) + iota((2 * HALF, HALF), 1) == 2 * HALF - 1).astype(F32)
    image[0] = jnp.concatenate([tt, tb.T], 0)
    image[1] = exact(jnp.concatenate([tb, bb], 0), reversal())

    def product(left, right):
        return jnp.sum((left * right).reshape(-1, 8, HALF), axis=0)

    def products(v_first, v_second, w_first, w_second):
        return product(v_first, w_first), product(v_second, w_second), product(v_first, w_second)

    def over_rows(sums):
        return tuple(jnp.sum(value, axis=0, keepdims=True) for value in sums)

    def turn(index, sums):
        cosine, factor = angles(*sums, index)
        found = None
        for c in range(2 * HALF // SOLVE_ROWS):
            where = pl.ds(c * SOLVE_ROWS, SOLVE_ROWS)
            fresh = []
            for ref in (basis, image):
                first, second = ref[0, where], ref[1, where]
                first, second = first * cosine + second * factor, second * cosine - first * factor
                first, second = shifted(first, second, 1)
                ref[0, where], ref[1, where] = first, second
                fresh += [first, second]
            part = products(*fresh)
            found = part if found is None else tuple(x + y for x, y in zip(found, part))
        return over_rows(found)

    sums = over_rows(products(basis[0], basis[1], image[0], image[1]))
    lax.fori_loop(0, INNER_ROUNDS, turn, sums)

    count = 2 * HALF - 1
    slot = iota((HALF, 2 * HALF), 0)
    natural = iota((HALF, 2 * HALF), 1)
    back = INNER_ROUNDS - slot
    place = jnp.where(slot == 0, count, jnp.where(back >= 0, back, back + count))
    first_place = natural == slot + INNER_ROUNDS
    second_place = natural == place

    high = []
    for part in zip(split(basis[0]), split(basis[1])):
        high.append((dot(part[0], first_place.astype(BF16)) + dot(part[1], second_place.astype(BF16))).astype(BF16))

    def turned():
        a, b = first_place.astype(F32), second_place.astype(F32)
        placed = exact(image[0], a) + exact(image[1], b)
        upper = exact_rows(basis[0], placed)
        lower = exact_rows(basis[1], placed)

        def block(columns):
            left = slice(columns * HALF, (columns + 1) * HALF)
            return exact(a[:, left].T, upper[:, left]) + exact(b[:, left].T, lower[:, left])

        return block(0), block(1)

    return high[0], high[1], turned


def times_basis(high, low, basis_high, basis_low):
    return dot(high, basis_high) + dot(low, basis_high) + dot(high, basis_low)


class Peers:
    def __init__(self, n):
        self.n, self.half = n, n // 2
        self.me = lax.axis_index("row")
        self.group, self.place = self.me // self.half, lax.rem(self.me, self.half)

    def at(self, other, offset):
        return lax.rem(self.group + other, 2) * self.half + lax.rem(self.place + self.half + offset, self.half)

    def each(self, action):
        def step(k, carry):
            offset = self.half // 2 + (1 - 2 * lax.rem(k, 2)) * ((k + 1) // 2)
            action(self.at(1, offset))
            action(self.at(0, offset))
            return carry

        lax.fori_loop(0, self.half - 1, step, 0)
        action(self.at(1, 0))

    def near(self, action):
        quarter = self.half // 4
        offsets = range(quarter - self.half // 2 + 1, quarter + 1)
        for offset in sorted(offsets, key=abs, reverse=True):
            action(self.at(1, offset))
            if offset:
                action(self.at(0, offset))


class Sum:
    def __init__(self, mine, parts, total, sems, peers, copies):
        self.mine, self.parts, self.total, self.sems, self.peers, self.copies = mine, parts, total, sems, peers, copies
        self.me = peers.me
        self.slices = peers.n // copies

    def slice_of(self, peer):
        if self.copies == 1:
            return peer
        half = self.peers.half
        return (peer // half) * (half // 2) + lax.rem(lax.rem(peer, half), half // 2)

    def drain(self, source, count, index):
        view = source.at[pl.ds(0, count)]
        pltpu.make_async_copy(view, view, self.sems.at[index]).wait()

    def scatter(self):
        self.peers.each(
            lambda peer: pltpu.make_async_remote_copy(
                src_ref=self.mine.at[self.slice_of(peer)],
                dst_ref=self.parts.at[self.me],
                send_sem=self.sems.at[0],
                recv_sem=self.sems.at[1],
                device_id={"row": peer},
                device_id_type=MESH,
            ).start()
        )
        self.parts[self.me] = self.mine[self.slice_of(self.me)]

    def add(self):
        self.drain(self.parts, self.peers.n - 1, 1)
        total = self.parts[0]
        for i in range(1, self.peers.n):
            total = total + self.parts[i]
        return total

    def gather(self, piece):
        own = self.slice_of(self.me)
        self.total[own] = piece
        (self.peers.each if self.copies == 1 else self.peers.near)(
            lambda peer: pltpu.make_async_remote_copy(
                src_ref=self.total.at[own],
                dst_ref=self.total.at[own],
                send_sem=self.sems.at[2],
                recv_sem=self.sems.at[3],
                device_id={"row": peer},
                device_id_type=MESH,
            ).start()
        )

    def wait(self):
        self.drain(self.total, self.slices - 1, 3)

    def finish(self):
        self.drain(self.parts, self.peers.n - 1, 0)
        self.drain(self.total, self.slices - 1, 2)


def kernel(
    n, cycle, x_hbm, t2, b2, w_ref,
    x, xh, xl, left, right, gram, got_rows, bases, got_bases,
    mine1, parts1, total1, mine2, parts2, total2,
    basis, image, blocks, got_blocks,
    load_sems, sums1, sums2, block_sems, base_sems, chunk_sems,
):
    col = lax.axis_index("col")
    chunks = x.shape[0] // CHUNK
    is_head, is_tail = col == 0, col == cycle - 1

    def load(c):
        where = pl.ds(c * CHUNK, CHUNK)
        return pltpu.make_async_copy(x_hbm.at[where], x.at[where], load_sems.at[c])

    for c in range(chunks):
        load(c).start()

    barrier = pltpu.get_barrier_semaphore()

    peers = Peers(n)
    peers.each(lambda peer: pl.semaphore_signal(barrier, inc=1, device_id={"row": peer}, device_id_type=MESH))

    @pl.when(jnp.logical_not(is_tail))
    def _():
        pl.semaphore_signal(barrier, inc=1, device_id={"col": col + 1}, device_id_type=MESH)

    @pl.when(jnp.logical_not(is_head))
    def _():
        pl.semaphore_signal(barrier, inc=1, device_id={"col": col - 1}, device_id_type=MESH)

    gram[...] = jnp.zeros_like(gram)
    for c in range(chunks):
        load(c).wait()
        where = pl.ds(c * CHUNK, CHUNK)
        high, low = split(x[where])
        xh[where] = high
        xl[where] = low
        gram[0] += dot_rows(high, high) + dot_rows(low, low)
        gram[1] += dot_rows(high, low)
    full = gram[0] + (gram[1] + gram[1].T)
    tt, tb, bb = full[:HALF, :HALF], full[:HALF, HALF:], full[HALF:, HALF:]
    below = iota((HALF, HALF), 0) >= iota((HALF, HALF), 1)
    eye = iota((HALF, HALF), 0) == iota((HALF, HALF), 1)
    folded = jnp.where(below, tt, bb)
    size1 = 2 * HALF // n
    mine1[:, :size1] = jnp.concatenate([tb, folded], 0).reshape(n, size1, HALF)
    corner = jnp.sum(jnp.where(eye, bb, 0.0), axis=0, keepdims=True)
    mine1[:, size1:] = jnp.broadcast_to(corner[None], (n, 1, HALF))

    inner = jnp.logical_not(jnp.logical_or(is_head, is_tail))

    @pl.when(inner)
    def _():
        pl.semaphore_wait(barrier, n + 1)

    @pl.when(jnp.logical_not(inner))
    def _():
        pl.semaphore_wait(barrier, n)

    def transfer(kind, source, target, sems, index):
        return pltpu.make_async_remote_copy(
            src_ref=source,
            dst_ref=target,
            send_sem=sems.at[0, index],
            recv_sem=sems.at[1, index],
            device_id={"col": col + 1 if kind == 0 else col - 1},
            device_id_type=MESH,
        )

    early = sum(EARLY)

    def rows_move(kind, c):
        where = pl.ds(c * CHUNK, CHUNK)
        if c < early:
            source, target = x.at[where], got_rows.at[kind, where]
        else:
            source, target = (left if kind else right).at[where], (b2 if kind else t2).at[where]
        return transfer(kind, source, target, chunk_sems, kind * chunks + c)

    def block_move(kind):
        return transfer(kind, blocks.at[kind], got_blocks.at[kind], block_sems, kind)

    def base_move(kind):
        return transfer(kind, bases.at[kind], got_bases.at[kind], base_sems, kind)

    def start(move):
        @pl.when(jnp.logical_not(is_tail))
        def _():
            move(0).start()

        @pl.when(jnp.logical_not(is_head))
        def _():
            move(1).start()

    def arrive(move):
        @pl.when(jnp.logical_not(is_head))
        def _():
            move(0).wait_recv()

        @pl.when(jnp.logical_not(is_tail))
        def _():
            move(1).wait_recv()

    def sent(move):
        @pl.when(jnp.logical_not(is_tail))
        def _():
            move(0).wait_send()

        @pl.when(jnp.logical_not(is_head))
        def _():
            move(1).wait_send()

    def rows(c):
        return lambda kind: rows_move(kind, c)

    sum1 = Sum(mine1, parts1, total1, sums1, peers, 1)
    sum1.scatter()
    for c in range(EARLY[0]):
        start(rows(c))
    piece = sum1.add()
    corner = piece[size1:]
    sum1.gather(piece[:size1])
    for c in range(EARLY[0], early):
        start(rows(c))

    @pl.when(is_head)
    def _():
        got_rows[0] = x[: early * CHUNK]

    @pl.when(is_tail)
    def _():
        got_rows[1] = x[: early * CHUNK]

    sum1.wait()
    whole = total1[...].reshape(2 * HALF, HALF)
    tb, folded = whole[:HALF], whole[HALF:]
    turned_fold = folded.T
    tt = jnp.where(below, folded, turned_fold)
    bb = jnp.where(below, turned_fold, folded)
    bb = jnp.where(eye, jnp.broadcast_to(corner, (HALF, HALF)), bb)

    basis_high, basis_low, turned = solve(tt, tb, bb, basis, image)

    whole_basis = basis_high.astype(F32) + basis_low.astype(F32)
    basis_top, basis_bottom = whole_basis[:, :HALF], whole_basis[:, HALF:]
    bases[0] = jnp.where(is_head, basis_bottom, basis_top)
    bases[1] = basis_bottom
    start(base_move)

    @pl.when(is_head)
    def _():
        got_bases[0] = basis_top

    @pl.when(is_tail)
    def _():
        got_bases[1] = basis_top

    for c in range(early, chunks):
        where = pl.ds(c * CHUNK, CHUNK)
        moved = times_basis(xh[where], xl[where], basis_high, basis_low)
        top, bottom = moved[:, :HALF], moved[:, HALF:]
        right[where] = jnp.where(is_head, bottom, top)
        left[where] = bottom

        @pl.when(is_head)
        def _():
            t2[where] = top

        @pl.when(is_tail)
        def _():
            b2[where] = top

        start(rows(c))

    tt, bb = turned()
    blocks[0] = jnp.where(is_head, bb, tt)
    blocks[1] = bb

    @pl.when(is_head)
    def _():
        got_blocks[0] = tt

    @pl.when(is_tail)
    def _():
        got_blocks[1] = tt

    start(block_move)

    for c in range(early):
        arrive(rows(c))
    arrive(base_move)
    got_top, got_bottom = split(got_bases[0]), split(got_bases[1])
    cross = jnp.zeros((HALF, HALF), F32)
    for c in range(chunks):
        where = pl.ds(c * CHUNK, CHUNK)
        if c < early:
            t2[where] = times_basis(*split(got_rows[0, where]), *got_top)
            b2[where] = times_basis(*split(got_rows[1, where]), *got_bottom)
        else:
            arrive(rows(c))
        th, tl = split(t2[where])
        bh, bl = split(b2[where])
        cross += dot_rows(th, bh) + dot_rows(tl, bh) + dot_rows(th, bl)
    mine2[...] = cross.reshape(mine2.shape)
    sum2 = Sum(mine2, parts2, total2, sums2, peers, 2)
    sum2.scatter()
    sum2.gather(sum2.add())
    arrive(block_move)
    sum2.wait()
    tb = total2[...].reshape(HALF, HALF)
    basis_high, basis_low, _ = solve(got_blocks[0], tb, got_blocks[1], basis, image)
    w_ref[0] = basis_high
    w_ref[1] = basis_low

    sum1.finish()
    sum2.finish()
    for c in range(chunks):
        sent(rows(c))
    sent(block_move)
    sent(base_move)


def last(t2, b2, w_ref, out, held, sems):
    chunks = held.shape[0] // CHUNK

    def store(c):
        where = pl.ds(c * CHUNK, CHUNK)
        return pltpu.make_async_copy(held.at[where], out.at[where], sems.at[c])

    for c in range(chunks):
        where = pl.ds(c * CHUNK, CHUNK)
        high, low = split(jnp.concatenate([t2[where], b2[where]], 1))
        held[where] = times_basis(high, low, w_ref[0], w_ref[1])
        store(c).start()
    for c in range(chunks):
        store(c).wait()


def local(n, cycle, snapshots):
    rows = snapshots.shape[0]
    chunks = rows // CHUNK
    dma = pltpu.SemaphoreType.DMA
    vmem = pl.BlockSpec(memory_space=pltpu.VMEM)
    size1, size2 = 2 * HALF // n, 2 * HALF // n
    t2, b2, w = pl.pallas_call(
        functools.partial(kernel, n, cycle),
        out_shape=[
            jax.ShapeDtypeStruct((rows, HALF), F32),
            jax.ShapeDtypeStruct((rows, HALF), F32),
            jax.ShapeDtypeStruct((2, 2 * HALF, 2 * HALF), BF16),
        ],
        in_specs=[pl.BlockSpec(memory_space=pltpu.HBM)],
        out_specs=[vmem] * 3,
        scratch_shapes=[
            pltpu.VMEM((rows, 2 * HALF), F32),
            pltpu.VMEM((rows, 2 * HALF), BF16),
            pltpu.VMEM((rows, 2 * HALF), BF16),
            pltpu.VMEM((rows, HALF), F32),
            pltpu.VMEM((rows, HALF), F32),
            pltpu.VMEM((2, 2 * HALF, 2 * HALF), F32),
            pltpu.VMEM((2, sum(EARLY) * CHUNK, 2 * HALF), F32),
            pltpu.VMEM((2, 2 * HALF, HALF), F32),
            pltpu.VMEM((2, 2 * HALF, HALF), F32),
            pltpu.VMEM((n, size1 + 1, HALF), F32),
            pltpu.VMEM((n, size1 + 1, HALF), F32),
            pltpu.VMEM((n, size1, HALF), F32),
            pltpu.VMEM((n // 2, size2, HALF), F32),
            pltpu.VMEM((n, size2, HALF), F32),
            pltpu.VMEM((n // 2, size2, HALF), F32),
            pltpu.VMEM((2, 2 * HALF, HALF), F32),
            pltpu.VMEM((2, 2 * HALF, HALF), F32),
            pltpu.VMEM((2, HALF, HALF), F32),
            pltpu.VMEM((2, HALF, HALF), F32),
            dma((chunks,)),
            dma((4,)),
            dma((4,)),
            dma((2, 2)),
            dma((2, 2)),
            dma((2, 2 * chunks)),
        ],
        compiler_params=pltpu.CompilerParams(
            collective_id=0, has_side_effects=True, vmem_limit_bytes=40 << 20
        ),
    )(pltpu.with_memory_space_constraint(snapshots, pltpu.HBM))
    return pl.pallas_call(
        last,
        out_shape=jax.ShapeDtypeStruct((rows, 2 * HALF), F32),
        in_specs=[vmem] * 3,
        out_specs=pl.BlockSpec(memory_space=pltpu.HBM),
        scratch_shapes=[pltpu.VMEM((rows, 2 * HALF), F32), dma((chunks,))],
        compiler_params=pltpu.CompilerParams(vmem_limit_bytes=24 << 20),
    )(t2, b2, w)


def solution(mesh):
    return jax.shard_map(
        functools.partial(local, mesh.shape["row"], mesh.shape["col"]),
        mesh=mesh,
        in_specs=(P("row", "col"),),
        out_specs=P("row", "col"),
        check_vma=False,
    )
```

time: 83 us -> 76.5 us (0.922)
  the two profiles are of different devices: /device:TPU:1 before, /device:TPU:8 now
where the time goes in v3:
time: 76.5 us; the launch traced here: 75.6 us
  Pallas kernels  75.6 us (99%)
    pallas_call x1, Pallas kernels, local(): pl.pallas_call(functools.partial(kernel, n, cycle), out_shape=[jax.ShapeD...  73.7 us
    pallas_call x1, Pallas kernels, local(): pl.pallas_call(last, out_shape=jax.ShapeDtypeStruct((rows, 2 * HALF), F32...  1.91 us

profile of v3, /device:TPU:8, one launch (start us, length us, event | category | flops | bytes accessed | tf_op | source)
XLA Modules:
  0.0 75.6 jit_solution(9003301390233811557)
XLA Ops:
  0.0 73.7 %shard_map.17 = (f32[2048,128]{1,0:T(8,128)S(1)}, f32[2048,128]{1,0:T(8,128)S(1)}, bf16[2,256,256]{2,1,0:T(8,128)(2,1)S(1)}) custom-call(f32[2048,256]{1,0:T(8,128)} %x_hbm.1), custom_call_target="tpu_custom_call" | custom-call | tf_op jit(solution)/shard_map/pallas_call | solution.py:473
  73.7 1.9 %shard_map.18 = f32[2048,256]{1,0:T(8,128)} custom-call(f32[2048,128]{1,0:T(8,128)S(1)} %get-tuple-element.8.t2, f32[2048,128]{1,0:T(8,128)S(1)} %get-tuple-element.9.b2, bf16[2,256,256]{2,1,0:T(8,128)(2,1)S(1)} %get-tuple-element.10.w_ref), custom_call_target="tpu_custom_call" | custom-call | tf_op jit(solution)/shard_map/pallas_call | solution.py:513

commit v4 on v3

--- a/solution.py
+++ b/solution.py
@@ -74,54 +74,79 @@
     return cosine, jnp.where(lead, -sine, sine)
 
 
-def solve(tt, tb, bb, basis, image):
+def fresh_basis(basis):
     basis[0] = (iota((2 * HALF, HALF), 0) == iota((2 * HALF, HALF), 1)).astype(F32)
     basis[1] = (iota((2 * HALF, HALF), 0) + iota((2 * HALF, HALF), 1) == 2 * HALF - 1).astype(F32)
-    image[0] = jnp.concatenate([tt, tb.T], 0)
-    image[1] = exact(jnp.concatenate([tb, bb], 0), reversal())
-
-    def product(left, right):
-        return jnp.sum((left * right).reshape(-1, 8, HALF), axis=0)
-
-    def products(v_first, v_second, w_first, w_second):
-        return product(v_first, w_first), product(v_second, w_second), product(v_first, w_second)
-
-    def over_rows(sums):
-        return tuple(jnp.sum(value, axis=0, keepdims=True) for value in sums)
-
-    def turn(index, sums):
-        cosine, factor = angles(*sums, index)
-        found = None
-        for c in range(2 * HALF // SOLVE_ROWS):
-            where = pl.ds(c * SOLVE_ROWS, SOLVE_ROWS)
-            fresh = []
-            for ref in (basis, image):
-                first, second = ref[0, where], ref[1, where]
-                first, second = first * cosine + second * factor, second * cosine - first * factor
-                first, second = shifted(first, second, 1)
-                ref[0, where], ref[1, where] = first, second
-                fresh += [first, second]
-            part = products(*fresh)
-            found = part if found is None else tuple(x + y for x, y in zip(found, part))
-        return over_rows(found)
-
-    sums = over_rows(products(basis[0], basis[1], image[0], image[1]))
-    lax.fori_loop(0, INNER_ROUNDS, turn, sums)
-
+
+
+def turn_columns(ref, where, cosine, factor):
+    first, second = ref[0, where], ref[1, where]
+    first, second = first * cosine + second * factor, second * cosine - first * factor
+    first, second = shifted(first, second, 1)
+    ref[0, where], ref[1, where] = first, second
+    return first, second
+
+
+def places():
     count = 2 * HALF - 1
     slot = iota((HALF, 2 * HALF), 0)
     natural = iota((HALF, 2 * HALF), 1)
     back = INNER_ROUNDS - slot
     place = jnp.where(slot == 0, count, jnp.where(back >= 0, back, back + count))
-    first_place = natural == slot + INNER_ROUNDS
-    second_place = natural == place
-
-    high = []
-    for part in zip(split(basis[0]), split(basis[1])):
-        high.append((dot(part[0], first_place.astype(BF16)) + dot(part[1], second_place.astype(BF16))).astype(BF16))
+    return natural == slot + INNER_ROUNDS, natural == place
+
+
+def natural_basis(basis):
+    first_place, second_place = places()
+    a, b = first_place.astype(BF16), second_place.astype(BF16)
+    return tuple((dot(x, a) + dot(y, b)).astype(BF16) for x, y in zip(split(basis[0]), split(basis[1])))
+
+
+def rebuild(turns, basis):
+    fresh_basis(basis)
+
+    def turn(index, carry):
+        cosine, factor = turns[0, pl.ds(index, 1)], turns[1, pl.ds(index, 1)]
+        for c in range(2 * HALF // SOLVE_ROWS):
+            turn_columns(basis, pl.ds(c * SOLVE_ROWS, SOLVE_ROWS), cosine, factor)
+        return carry
+
+    lax.fori_loop(0, INNER_ROUNDS, turn, 0)
+    return natural_basis(basis)
+
+
+def solve(tt, tb, bb, basis, image, turns=None):
+    fresh_basis(basis)
+    image[0] = jnp.concatenate([tt, tb.T], 0)
+    image[1] = exact(jnp.concatenate([tb, bb], 0), reversal())
+
+    def product(left, right):
+        return jnp.sum((left * right).reshape(-1, 8, HALF), axis=0)
+
+    def products(v_first, v_second, w_first, w_second):
+        return product(v_first, w_first), product(v_second, w_second), product(v_first, w_second)
+
+    def over_rows(sums):
+        return tuple(jnp.sum(value, axis=0, keepdims=True) for value in sums)
+
+    def turn(index, sums):
+        cosine, factor = angles(*sums, index)
+        if turns is not None:
+            turns[0, pl.ds(index, 1)] = cosine
+            turns[1, pl.ds(index, 1)] = factor
+        found = None
+        for c in range(2 * HALF // SOLVE_ROWS):
+            where = pl.ds(c * SOLVE_ROWS, SOLVE_ROWS)
+            part = products(*turn_columns(basis, where, cosine, factor), *turn_columns(image, where, cosine, factor))
+            found = part if found is None else tuple(x + y for x, y in zip(found, part))
+        return over_rows(found)
+
+    sums = over_rows(products(basis[0], basis[1], image[0], image[1]))
+    lax.fori_loop(0, INNER_ROUNDS, turn, sums)
+    high, low = natural_basis(basis)
 
     def turned():
-        a, b = first_place.astype(F32), second_place.astype(F32)
+        a, b = (place.astype(F32) for place in places())
         placed = exact(image[0], a) + exact(image[1], b)
         upper = exact_rows(basis[0], placed)
         lower = exact_rows(basis[1], placed)
@@ -132,7 +157,7 @@
 
         return block(0), block(1)
 
-    return high[0], high[1], turned
+    return high, low, turned
 
 
 def times_basis(high, low, basis_high, basis_low):
@@ -227,10 +252,10 @@
 
 def kernel(
     n, cycle, x_hbm, t2, b2, w_ref,
-    x, xh, xl, left, right, gram, got_rows, bases, got_bases,
+    x, xh, xl, left, right, gram, got_rows, turns, got_turns, other,
     mine1, parts1, total1, mine2, parts2, total2,
     basis, image, blocks, got_blocks,
-    load_sems, sums1, sums2, block_sems, base_sems, chunk_sems,
+    load_sems, sums1, sums2, block_sems, turn_sems, chunk_sems,
 ):
     col = lax.axis_index("col")
     chunks = x.shape[0] // CHUNK
@@ -308,8 +333,8 @@
     def block_move(kind):
         return transfer(kind, blocks.at[kind], got_blocks.at[kind], block_sems, kind)
 
-    def base_move(kind):
-        return transfer(kind, bases.at[kind], got_bases.at[kind], base_sems, kind)
+    def turn_move(kind):
+        return transfer(kind, turns, got_turns.at[kind], turn_sems, kind)
 
     def start(move):
         @pl.when(jnp.logical_not(is_tail))
@@ -367,21 +392,18 @@
     bb = jnp.where(below, turned_fold, folded)
     bb = jnp.where(eye, jnp.broadcast_to(corner, (HALF, HALF)), bb)
 
-    basis_high, basis_low, turned = solve(tt, tb, bb, basis, image)
-
-    whole_basis = basis_high.astype(F32) + basis_low.astype(F32)
-    basis_top, basis_bottom = whole_basis[:, :HALF], whole_basis[:, HALF:]
-    bases[0] = jnp.where(is_head, basis_bottom, basis_top)
-    bases[1] = basis_bottom
-    start(base_move)
+    turns[...] = jnp.zeros_like(turns)
+    basis_high, basis_low, turned = solve(tt, tb, bb, basis, image, turns)
+
+    start(turn_move)
 
     @pl.when(is_head)
     def _():
-        got_bases[0] = basis_top
+        got_turns[0] = turns[...]
 
     @pl.when(is_tail)
     def _():
-        got_bases[1] = basis_top
+        got_turns[1] = turns[...]
 
     for c in range(early, chunks):
         where = pl.ds(c * CHUNK, CHUNK)
@@ -414,10 +436,15 @@
 
     start(block_move)
 
+    arrive(turn_move)
+    got_top = [
+        jnp.where(col == 1, part[:, HALF:], part[:, :HALF]) for part in rebuild(got_turns.at[0], other)
+    ]
+    got_bottom = [
+        jnp.where(is_tail, part[:, :HALF], part[:, HALF:]) for part in rebuild(got_turns.at[1], other)
+    ]
     for c in range(early):
         arrive(rows(c))
-    arrive(base_move)
-    got_top, got_bottom = split(got_bases[0]), split(got_bases[1])
     cross = jnp.zeros((HALF, HALF), F32)
     for c in range(chunks):
         where = pl.ds(c * CHUNK, CHUNK)
@@ -445,7 +472,7 @@
     for c in range(chunks):
         sent(rows(c))
     sent(block_move)
-    sent(base_move)
+    sent(turn_move)
 
 
 def last(t2, b2, w_ref, out, held, sems):
@@ -487,7 +514,8 @@
             pltpu.VMEM((rows, HALF), F32),
             pltpu.VMEM((2, 2 * HALF, 2 * HALF), F32),
             pltpu.VMEM((2, sum(EARLY) * CHUNK, 2 * HALF), F32),
-            pltpu.VMEM((2, 2 * HALF, HALF), F32),
+            pltpu.VMEM((2, 16, HALF), F32),
+            pltpu.VMEM((2, 2, 16, HALF), F32),
             pltpu.VMEM((2, 2 * HALF, HALF), F32),
             pltpu.VMEM((n, size1 + 1, HALF), F32),
             pltpu.VMEM((n, size1 + 1, HALF), F32),

time: 76.5 us -> 73.9 us (0.966)
  Pallas kernels: 75.6 us -> 72.7 us
    pallas_call x1, Pallas kernels: 73.7 us -> 70.8 us  [local(): pl.pallas_call(functools.partial(kernel, n, cycle), out_shape=[jax.ShapeD...]
where the time goes in v4:
time: 73.9 us; the launch traced here: 72.7 us
  Pallas kernels  72.7 us (98%)
    pallas_call x1, Pallas kernels, local(): pl.pallas_call(functools.partial(kernel, n, cycle), out_shape=[jax.ShapeD...  70.8 us
    pallas_call x1, Pallas kernels, local(): pl.pallas_call(last, out_shape=jax.ShapeDtypeStruct((rows, 2 * HALF), F32...  1.91 us

profile of v4, /device:TPU:8, one launch (start us, length us, event | category | flops | bytes accessed | tf_op | source)
XLA Modules:
  0.0 72.7 jit_solution(8254940604450325376)
XLA Ops:
  0.0 70.8 %shard_map.17 = (f32[2048,128]{1,0:T(8,128)S(1)}, f32[2048,128]{1,0:T(8,128)S(1)}, bf16[2,256,256]{2,1,0:T(8,128)(2,1)S(1)}) custom-call(f32[2048,256]{1,0:T(8,128)} %x_hbm.1), custom_call_target="tpu_custom_call" | custom-call | tf_op jit(solution)/shard_map/pallas_call | solution.py:500
  70.8 1.9 %shard_map.18 = f32[2048,256]{1,0:T(8,128)} custom-call(f32[2048,128]{1,0:T(8,128)S(1)} %get-tuple-element.8.t2, f32[2048,128]{1,0:T(8,128)S(1)} %get-tuple-element.9.b2, bf16[2,256,256]{2,1,0:T(8,128)(2,1)S(1)} %get-tuple-element.10.w_ref), custom_call_target="tpu_custom_call" | custom-call | tf_op jit(solution)/shard_map/pallas_call | solution.py:541

commit v5 on v4

--- a/solution.py
+++ b/solution.py
@@ -9,8 +9,8 @@
 
 INNER_ROUNDS = 10
 HALF = 128
-CHUNK = 256
-EARLY = (1, 2)
+CHUNK = 128
+EARLY = (3,3)
 SOLVE_ROWS = 64
 MESH = pl.DeviceIdType.MESH
 F32 = jnp.float32
@@ -65,12 +65,14 @@
     height = jnp.where(gap_lead >= 0, -2.0, 2.0) * cross
     width = jnp.abs(gap)
     big = jnp.maximum(width, jnp.abs(height))
-    scale = 1.0 / jnp.where(big > 0, big, 1.0)
-    width, height = width * scale, height * scale
-    total = width + jnp.sqrt(width * width + height * height)
-    tangent = height / jnp.where(big > 0, total, 1.0)
-    cosine = lax.rsqrt(1.0 + tangent * tangent)
-    sine = tangent * cosine
+    some = big > 0
+    scale = 1.0 / jnp.where(some, big, 1.0)
+    width, height = jnp.where(some, width * scale, 1.0), height * scale
+    inverse = lax.rsqrt(width * width + height * height)
+    squared = 0.5 + 0.5 * (width * inverse)
+    inverse_cosine = lax.rsqrt(squared)
+    cosine = squared * inverse_cosine
+    sine = (0.5 * height * inverse) * inverse_cosine
     return cosine, jnp.where(lead, -sine, sine)
 
 
@@ -123,26 +125,34 @@
     def product(left, right):
         return jnp.sum((left * right).reshape(-1, 8, HALF), axis=0)
 
-    def products(v_first, v_second, w_first, w_second):
-        return product(v_first, w_first), product(v_second, w_second), product(v_first, w_second)
-
-    def over_rows(sums):
-        return tuple(jnp.sum(value, axis=0, keepdims=True) for value in sums)
-
-    def turn(index, sums):
-        cosine, factor = angles(*sums, index)
+    def over_rows(value):
+        return jnp.sum(value, axis=0, keepdims=True)
+
+    def turn(index, entries):
+        diag_first, diag_second, cross = entries
+        cosine, factor = angles(diag_first, diag_second, cross, index)
         if turns is not None:
             turns[0, pl.ds(index, 1)] = cosine
             turns[1, pl.ds(index, 1)] = factor
         found = None
         for c in range(2 * HALF // SOLVE_ROWS):
             where = pl.ds(c * SOLVE_ROWS, SOLVE_ROWS)
-            part = products(*turn_columns(basis, where, cosine, factor), *turn_columns(image, where, cosine, factor))
-            found = part if found is None else tuple(x + y for x, y in zip(found, part))
-        return over_rows(found)
-
-    sums = over_rows(products(basis[0], basis[1], image[0], image[1]))
-    lax.fori_loop(0, INNER_ROUNDS, turn, sums)
+            v_first, _ = turn_columns(basis, where, cosine, factor)
+            _, w_second = turn_columns(image, where, cosine, factor)
+            part = product(v_first, w_second)
+            found = part if found is None else found + part
+        keep, take, mix = cosine * cosine, factor * factor, 2.0 * cosine * factor * cross
+        diag_first, diag_second = shifted(
+            keep * diag_first + take * diag_second + mix, keep * diag_second + take * diag_first - mix, 1
+        )
+        return diag_first, diag_second, over_rows(found)
+
+    start = (
+        over_rows(product(basis[0], image[0])),
+        over_rows(product(basis[1], image[1])),
+        over_rows(product(basis[0], image[1])),
+    )
+    lax.fori_loop(0, INNER_ROUNDS, turn, start)
     high, low = natural_basis(basis)
 
     def turned():
@@ -251,8 +261,8 @@
 
 
 def kernel(
-    n, cycle, x_hbm, t2, b2, w_ref,
-    x, xh, xl, left, right, gram, got_rows, turns, got_turns, other,
+    n, cycle, x_hbm, high_ref, low_ref, w_ref,
+    x, t2, b2, xh, xl, left, right, gram, got_rows, turns, got_turns, other,
     mine1, parts1, total1, mine2, parts2, total2,
     basis, image, blocks, got_blocks,
     load_sems, sums1, sums2, block_sems, turn_sems, chunk_sems,
@@ -434,8 +444,6 @@
     def _():
         got_blocks[1] = tt
 
-    start(block_move)
-
     arrive(turn_move)
     got_top = [
         jnp.where(col == 1, part[:, HALF:], part[:, :HALF]) for part in rebuild(got_turns.at[0], other)
@@ -455,10 +463,13 @@
             arrive(rows(c))
         th, tl = split(t2[where])
         bh, bl = split(b2[where])
+        high_ref[where, :HALF], high_ref[where, HALF:] = th, bh
+        low_ref[where, :HALF], low_ref[where, HALF:] = tl, bl
         cross += dot_rows(th, bh) + dot_rows(tl, bh) + dot_rows(th, bl)
     mine2[...] = cross.reshape(mine2.shape)
     sum2 = Sum(mine2, parts2, total2, sums2, peers, 2)
     sum2.scatter()
+    start(block_move)
     sum2.gather(sum2.add())
     arrive(block_move)
     sum2.wait()
@@ -475,7 +486,7 @@
     sent(turn_move)
 
 
-def last(t2, b2, w_ref, out, held, sems):
+def last(high_ref, low_ref, w_ref, out, held, sems):
     chunks = held.shape[0] // CHUNK
 
     def store(c):
@@ -484,8 +495,7 @@
 
     for c in range(chunks):
         where = pl.ds(c * CHUNK, CHUNK)
-        high, low = split(jnp.concatenate([t2[where], b2[where]], 1))
-        held[where] = times_basis(high, low, w_ref[0], w_ref[1])
+        held[where] = times_basis(high_ref[where], low_ref[where], w_ref[0], w_ref[1])
         store(c).start()
     for c in range(chunks):
         store(c).wait()
@@ -497,17 +507,19 @@
     dma = pltpu.SemaphoreType.DMA
     vmem = pl.BlockSpec(memory_space=pltpu.VMEM)
     size1, size2 = 2 * HALF // n, 2 * HALF // n
-    t2, b2, w = pl.pallas_call(
+    high, low, w = pl.pallas_call(
         functools.partial(kernel, n, cycle),
         out_shape=[
-            jax.ShapeDtypeStruct((rows, HALF), F32),
-            jax.ShapeDtypeStruct((rows, HALF), F32),
+            jax.ShapeDtypeStruct((rows, 2 * HALF), BF16),
+            jax.ShapeDtypeStruct((rows, 2 * HALF), BF16),
             jax.ShapeDtypeStruct((2, 2 * HALF, 2 * HALF), BF16),
         ],
         in_specs=[pl.BlockSpec(memory_space=pltpu.HBM)],
         out_specs=[vmem] * 3,
         scratch_shapes=[
             pltpu.VMEM((rows, 2 * HALF), F32),
+            pltpu.VMEM((rows, HALF), F32),
+            pltpu.VMEM((rows, HALF), F32),
             pltpu.VMEM((rows, 2 * HALF), BF16),
             pltpu.VMEM((rows, 2 * HALF), BF16),
             pltpu.VMEM((rows, HALF), F32),
@@ -545,7 +557,7 @@
         out_specs=pl.BlockSpec(memory_space=pltpu.HBM),
         scratch_shapes=[pltpu.VMEM((rows, 2 * HALF), F32), dma((chunks,))],
         compiler_params=pltpu.CompilerParams(vmem_limit_bytes=24 << 20),
-    )(t2, b2, w)
+    )(high, low, w)
 
 
 def solution(mesh):

time: 73.9 us -> 72.8 us (0.985); the launches traced: 72.7 us -> 72.6 us
  no operation moved by 1% of the time
where the time goes in v5:
time: 72.8 us; the launch traced here: 72.6 us
  Pallas kernels  72.6 us (100%)
    pallas_call x1, Pallas kernels, local(): pl.pallas_call(functools.partial(kernel, n, cycle), out_shape=[jax.ShapeD...  70.8 us
    pallas_call x1, Pallas kernels, local(): pl.pallas_call(last, out_shape=jax.ShapeDtypeStruct((rows, 2 * HALF), F32...  1.83 us

profile of v5, /device:TPU:8, one launch (start us, length us, event | category | flops | bytes accessed | tf_op | source)
XLA Modules:
  0.0 72.6 jit_solution(3861044349243833003)
XLA Ops:
  0.0 70.8 %shard_map.17 = (bf16[2048,256]{1,0:T(8,128)(2,1)S(1)}, bf16[2048,256]{1,0:T(8,128)(2,1)S(1)}, bf16[2,256,256]{2,1,0:T(8,128)(2,1)S(1)}) custom-call(f32[2048,256]{1,0:T(8,128)} %x_hbm.1), custom_call_target="tpu_custom_call" | custom-call | tf_op jit(solution)/shard_map/pallas_call | solution.py:510
  70.8 1.8 %shard_map.18 = f32[2048,256]{1,0:T(8,128)} custom-call(bf16[2048,256]{1,0:T(8,128)(2,1)S(1)} %get-tuple-element.8.high_ref, bf16[2048,256]{1,0:T(8,128)(2,1)S(1)} %get-tuple-element.9.low_ref, bf16[2,256,256]{2,1,0:T(8,128)(2,1)S(1)} %get-tuple-element.10.w_ref), custom_call_target="tpu_custom_call" | custom-call | tf_op jit(solution)/shard_map/pallas_call | solution.py:553

commit v6 on v5

--- a/solution.py
+++ b/solution.py
@@ -10,7 +10,7 @@
 INNER_ROUNDS = 10
 HALF = 128
 CHUNK = 128
-EARLY = (3,3)
+EARLY = (4,2)
 SOLVE_ROWS = 64
 MESH = pl.DeviceIdType.MESH
 F32 = jnp.float32
@@ -117,10 +117,15 @@
     return natural_basis(basis)
 
 
-def solve(tt, tb, bb, basis, image, turns=None):
+def prepare(tt, bb, basis, image):
     fresh_basis(basis)
-    image[0] = jnp.concatenate([tt, tb.T], 0)
-    image[1] = exact(jnp.concatenate([tb, bb], 0), reversal())
+    image[0, :HALF] = tt
+    image[1, HALF:] = exact(bb, reversal())
+
+
+def solve(tb, basis, image, turns=None):
+    image[0, HALF:] = tb.T
+    image[1, :HALF] = exact(tb, reversal())
 
     def product(left, right):
         return jnp.sum((left * right).reshape(-1, 8, HALF), axis=0)
@@ -403,7 +408,8 @@
     bb = jnp.where(eye, jnp.broadcast_to(corner, (HALF, HALF)), bb)
 
     turns[...] = jnp.zeros_like(turns)
-    basis_high, basis_low, turned = solve(tt, tb, bb, basis, image, turns)
+    prepare(tt, bb, basis, image)
+    basis_high, basis_low, turned = solve(tb, basis, image, turns)
 
     start(turn_move)
 
@@ -472,9 +478,10 @@
     start(block_move)
     sum2.gather(sum2.add())
     arrive(block_move)
+    prepare(got_blocks[0], got_blocks[1], basis, image)
     sum2.wait()
     tb = total2[...].reshape(HALF, HALF)
-    basis_high, basis_low, _ = solve(got_blocks[0], tb, got_blocks[1], basis, image)
+    basis_high, basis_low, _ = solve(tb, basis, image)
     w_ref[0] = basis_high
     w_ref[1] = basis_low
 

time: 72.8 us -> 72.7 us (level)
  no operation moved by 1% of the time
where the time goes in v6:
time: 72.7 us; the launch traced here: 72.3 us
  Pallas kernels  72.3 us (99%)
    pallas_call x1, Pallas kernels, local(): pl.pallas_call(functools.partial(kernel, n, cycle), out_shape=[jax.ShapeD...  70.4 us
    pallas_call x1, Pallas kernels, local(): pl.pallas_call(last, out_shape=jax.ShapeDtypeStruct((rows, 2 * HALF), F32...  1.83 us

profile of v6, /device:TPU:8, one launch (start us, length us, event | category | flops | bytes accessed | tf_op | source)
XLA Modules:
  0.0 72.3 jit_solution(17934660639091856060)
XLA Ops:
  0.0 70.4 %shard_map.17 = (bf16[2048,256]{1,0:T(8,128)(2,1)S(1)}, bf16[2048,256]{1,0:T(8,128)(2,1)S(1)}, bf16[2,256,256]{2,1,0:T(8,128)(2,1)S(1)}) custom-call(f32[2048,256]{1,0:T(8,128)} %x_hbm.1), custom_call_target="tpu_custom_call" | custom-call | tf_op jit(solution)/shard_map/pallas_call | solution.py:517
  70.5 1.8 %shard_map.18 = f32[2048,256]{1,0:T(8,128)} custom-call(bf16[2048,256]{1,0:T(8,128)(2,1)S(1)} %get-tuple-element.8.high_ref, bf16[2048,256]{1,0:T(8,128)(2,1)S(1)} %get-tuple-element.9.low_ref, bf16[2,256,256]{2,1,0:T(8,128)(2,1)S(1)} %get-tuple-element.10.w_ref), custom_call_target="tpu_custom_call" | custom-call | tf_op jit(solution)/shard_map/pallas_call | solution.py:560
